TPU v7x, 256 devices: a whole 4x4x8 slice. The times are simulated.
256 devices in a mesh: seg: 4 (over y_hi, core), mic: 64 (over z, x, y_lo).
Axes of the slice: x: 4, y: 4 (y_hi: 2, y_lo: 2; y = y_hi * 2 + y_lo), z: 8, core: 2. Of those that a mesh axis runs over, the one named last changes fastest.
Arguments:
- time_data: bfloat16 [128, 4096, 1024], P('seg', 'mic'), may hold values from -6 to 6
- order_bin: int32 [1], replicated, may hold values from 32 to 203
- mic_pos: int32 [3, 4096], replicated, may hold values from -2000 to 2000
- grid_pos: int32 [3, 131072], P(None, 'mic'), may hold values from -1500 to 1500
Outputs:
- beam_power: float32 [64, 2048], P('mic', 'seg')
All inputs are finite; a program needn't handle non-finite values.
Results may differ from a plain program's by a relative error of at most 0.00083.
Values may be sent and summed in bfloat16 or wider, within the bound.
A program may use at most 256 MiB of HBM per device.

v0:
```python
import math
import jax
import jax.numpy as jnp
from jax import lax
from jax.sharding import PartitionSpec as P


def spectral_table(order_value, samples):
    times = jnp.arange(samples, dtype=jnp.int32)
    turned = order_value * times % samples
    angle = turned.astype(jnp.float32) * (2.0 * math.pi / samples)
    window = 0.5 - 0.5 * jnp.cos(times.astype(jnp.float32) * (2.0 * math.pi / samples))
    return jnp.stack([window * jnp.cos(angle), -(window * jnp.sin(angle))]).astype(jnp.bfloat16)


def stacked_left(spectra):
    real_part = spectra[0]
    imag_part = spectra[1]
    upper = jnp.concatenate([real_part, -imag_part], axis=1)
    lower = jnp.concatenate([imag_part, real_part], axis=1)
    return jnp.concatenate([upper, lower], axis=0)


def beam_block(left, mic_part, points, wave):
    offsets = (points[:, None, :] - mic_part[:, :, None]).astype(jnp.float32) * 0.001
    distance = jnp.sqrt(offsets[0] * offsets[0] + offsets[1] * offsets[1] + offsets[2] * offsets[2])
    phase = wave * distance
    steering = jnp.concatenate([jnp.cos(phase), jnp.sin(phase)], axis=0).astype(jnp.bfloat16)
    return jnp.dot(left, steering, preferred_element_type=jnp.float32)


def make_folder(points, mic_pos, wave):

    def accumulate(carry, piece, start):
        left = stacked_left(piece)
        return beam_block(left, mic_pos, points, wave)

    return accumulate


def shards(time_data, order_bin, mic_pos, grid_pos):
    seg_dev = time_data.shape[0]
    mic_dev = time_data.shape[1]
    samples = time_data.shape[2]
    table = spectral_table(order_bin[0], samples)
    rows = time_data.reshape(seg_dev * mic_dev, samples)
    spec = jnp.dot(rows, table.T, preferred_element_type=jnp.float32)
    spectra = spec.T.reshape(2, seg_dev, mic_dev).astype(jnp.bfloat16)
    wave = (
        order_bin[0].astype(jnp.float32)
        * jnp.float32(2.0 * math.pi * 51200.0 / 343.0)
        / jnp.float32(samples)
    )
    seg_count = lax.axis_size("seg")
    seg_total = seg_count * seg_dev
    mic_total = lax.axis_size("mic") * mic_dev
    denom = jnp.float32(seg_total * mic_total * 0.375 * samples)
    slab_width = grid_pos.shape[1]
    own_width = slab_width // seg_count
    folder = make_folder(grid_pos, mic_pos, wave)
    empty = jnp.zeros((2 * seg_dev, slab_width), jnp.float32)
    beams = folder(empty, lax.all_gather(spectra, "mic", axis=2, tiled=True), jnp.int32(0))
    partial_power = jnp.sum(beams * beams, axis=0) / denom
    beam_power = lax.psum_scatter(partial_power, "seg", scatter_dimension=0, tiled=True)
    return beam_power.reshape(1, own_width)


def solution(mesh):
    placed = (P("seg", "mic", None), P(), P(), P(None, "mic"))
    return jax.shard_map(
        shards, mesh=mesh, in_specs=placed, out_specs=P("mic", "seg"), check_vma=False
    )
```

profile of v0, /device:TPU:1, one launch (start us, length us, event | category | flops | bytes accessed | tf_op | source)
XLA Modules:
  0.0 471.5 jit_solution(192973803990093008)
XLA Ops:
  0.0 32.1 %convert_multiply_fusion = f32[3,4096,2048]{2,1,0:T(8,128)} fusion(s32[3,4096]{1,0:T(4,128)} %param.6, s32[3,2048]{1,0:T(4,128)} %param.7), kind=kLoop, calls=%fused_computation | loop fusion | flops 75497472 | bytes 100737024 | tf_op jit(solution)/shard_map/mul | solution.py:25
  32.8 124.3 %fusion.8 = (bf16[4096,2048]{1,0:T(8,128)(2,1)}, f32[1,4096,2048]{2,1,0:T(8,128)S(1)}) fusion(f32[3,4096,2048]{2,1,0:T(8,128)} %convert_multiply_fusion, f32[]{:T(128)S(6)} %div.9), kind=kLoop, calls=%fused_computation.14 | loop fusion | flops 58720256 | bytes 150994944 | tf_op jit(solution)/shard_map/convert
  157.1 0.0 copy-start
  157.1 108.2 %fusion.9 = bf16[4096,2048]{1,0:T(8,128)(2,1)} fusion(f32[1,4096,2048]{2,1,0:T(8,128)S(1)} %get-tuple-element.6), kind=kLoop, calls=%fused_computation.15 | loop fusion | flops 8388608 | bytes 50331648 | tf_op jit(solution)/shard_map/convert.1
  265.3 0.3 negate_convert_fusion
  265.5 0.0 copy-done
  265.5 1.7 convolution_convert_fusion
  267.3 0.1 copy.6
  267.4 144.7 %all_gather.3 = bf16[2,32,4096]{1,0,2:T(2,128)(2,1)S(1)} all-gather(bf16[2,32,64]{1,0,2:T(2,128)(2,1)S(1)} %copy.6), channel_id=1, replica_groups=mesh['seg'=4,'mic'=64] {'mic'}, dimensions={2}, use_global_device_ids=true | all-gather | bytes 532480 | tf_op jit(solution)/shard_map/all_gather | solution.py:62
  412.1 3.8 fusion.31
  415.9 0.0 copy-start.1
  415.9 4.5 copy.9
  420.4 2.1 copy.10
  422.5 12.7 %fusion.13 = f32[2048]{0:T(1024)S(1)} fusion(bf16[4096,2048]{1,0:T(8,128)(2,1)} %fusion.9, bf16[4096,2048]{1,0:T(8,128)(2,1)} %get-tuple-element.5, bf16[32,4096]{1,0:T(8,128)(2,1)S(1)} %bitcast.17, bf16[32,4096]{1,0:T(8,128)(2,1)S(1)} %bitcast.16, bf16[32,4096]{1,0:T(8,128)(2,1)S(1)} %bitcast_negate_fusion), kind=kOutput, calls=%fused_computation.17 | convolution fusion | flops 2219046912 | bytes 34349056 | tf_op jit(solution)/shard_map/dot_general | solution.py:29
  435.3 34.3 %all-reduce = f32[2048]{0:T(1024)S(1)} all-reduce(f32[2048]{0:T(1024)S(1)} %broadcast_multiply_fusion), channel_id=2, replica_groups=mesh['seg'=4,'mic'=64] {'seg'}, use_global_device_ids=true, to_apply=%region_1.2.clone | all-reduce | flops 2048 | bytes 16384
  469.6 0.0 copy-done.1
  469.6 0.6 dynamic-slice
  470.9 0.7 dynamic-slice.1
  (2 shorter events, 0.0 us)
Async XLA Ops:
  157.1 108.5 %copy-start = (bf16[32,64,1024]{2,1,0:T(8,128)(2,1)S(1)}, bf16[32,64,1024]{2,1,0:T(8,128)(2,1)}, u32[]{:S(2)}) copy-start(bf16[32,64,1024]{2,1,0:T(8,128)(2,1)} %param.4) | copy-start | bytes 12582916
  415.9 53.7 %copy-start.1 = (u32[256]{0:T(256)S(1)}, u32[256]{0:T(256)}, u32[]{:S(2)}) copy-start(u32[256]{0:T(256)} %constant.33) | copy-start | bytes 3076
where the time goes:
time: 472 us
  other arithmetic  265 us (56%)
  blocking collectives  179 us (38%)
  matrix products  14.5 us (3%)
  local copies, waits for them, and re-layouts  11.7 us (2%)
    another operation x3, other arithmetic  233 us
    all_gather x1, blocking collectives, shards(): lax.all_gather(spectra, 'mic', axis=2, tiled=True)  145 us
    unnamed x1, blocking collectives  34.3 us
    mul x1, other arithmetic, beam_block(): (points[:, None, :] - mic_part[:, :, None]).astype(jnp.float32) * 0.001  32.1 us
    dot_general x1, matrix products, beam_block(): return jnp.dot(left, steering, preferred_element_type=jnp.float32)  12.7 us

commit v1 on v0

--- a/solution.py
+++ b/solution.py
@@ -59,7 +59,13 @@
     own_width = slab_width // seg_count
     folder = make_folder(grid_pos, mic_pos, wave)
     empty = jnp.zeros((2 * seg_dev, slab_width), jnp.float32)
-    beams = folder(empty, lax.all_gather(spectra, "mic", axis=2, tiled=True), jnp.int32(0))
+    beams = folder(
+        empty,
+        jnp.concatenate(
+            lax.all_to_all(jnp.stack([spectra] * lax.axis_size("mic"), 0), "mic", 0, 0), 2
+        ),
+        jnp.int32(0),
+    )
     partial_power = jnp.sum(beams * beams, axis=0) / denom
     beam_power = lax.psum_scatter(partial_power, "seg", scatter_dimension=0, tiled=True)
     return beam_power.reshape(1, own_width)

time: 472 us -> 311 us (0.66)
  blocking collectives: 179 us -> 7.6 us
  starting transfers between devices: 0 us -> 13.7 us
  local copies, waits for them, and re-layouts: 11.7 us -> 5.15 us
    all_gather x1 -> x0, blocking collectives: 145 us -> none  [shards(): lax.all_gather(spectra, 'mic', axis=2, tiled=True)]
    unnamed x1, blocking collectives: 34.3 us -> 7.6 us
    all_to_all x0 -> x1, starting transfers between devices: none -> 13.7 us  [shards(): lax.all_to_all(jnp.stack([spectra] * lax.axis_size('mic'), 0), 'mic', 0, 0)]
  transfers between devices with their start and end apart: 0 -> 1, of which waited for: 0 -> 0; matrix products, arithmetic and copies ran while one was open for 0% -> 86% of each run, Pallas kernels for 0% -> 0%
where the time goes in v1:
time: 311 us; the launch traced here: 309 us
  other arithmetic  265 us (85%)
  matrix products  16.6 us (5%)
  starting transfers between devices  13.7 us (4%)
  blocking collectives  7.6 us (2%)
  local copies, waits for them, and re-layouts  5.15 us (2%)
    another operation x3, other arithmetic  233 us
    mul x1, other arithmetic, beam_block(): (points[:, None, :] - mic_part[:, :, None]).astype(jnp.float32) * 0.001  32.1 us
    all_to_all x1, starting transfers between devices, shards(): lax.all_to_all(jnp.stack([spectra] * lax.axis_size('mic'), 0), 'mic', 0, 0)  13.7 us
    dot_general x1, matrix products, beam_block(): return jnp.dot(left, steering, preferred_element_type=jnp.float32)  12.7 us
    unnamed x1, blocking collectives  7.6 us
  transfers between devices with their start and end apart: 1, of which 0 were waited for; matrix products, arithmetic and copies ran while one was open for 86% of the time, Pallas kernels for 0%

profile of v1, /device:TPU:1, one launch (start us, length us, event | category | flops | bytes accessed | tf_op | source)
XLA Modules:
  0.0 309.4 jit_solution(7771757319805510224)
XLA Ops:
  0.7 0.3 negate_convert_fusion
  0.9 3.9 %convolution_convert_fusion = bf16[2,32,64]{2,0,1:T(2,128)(2,1)S(1)} fusion(bf16[32,64,1024]{2,1,0:T(8,128)(2,1)} %param.4, bf16[1,1024]{1,0:T(2,128)(2,1)S(1)} %get-tuple-element.9, bf16[1,1024]{1,0:T(2,128)(2,1)S(1)} %get-tuple-element.10), kind=kOutput, calls=%fused_computation.18 | convolution fusion | flops 8400896 | bytes 4206592 | tf_op jit(solution)/shard_map/dot_general | solution.py:47
  4.8 0.3 stack.6
  5.1 1.6 reshape.116
  6.7 13.7 %all-to-all-start = ((bf16[64,2,2048]{2,1,0:T(2,128)(2,1)}), bf16[64,2,2048]{2,1,0:T(2,128)(2,1)S(1)}, u32[]{:S(2)}, u32[]{:S(2)}) async-start(bf16[64,2,2048]{2,1,0:T(2,128)(2,1)} %reshape.116), calls=%async_computation | async-start | bytes 1048576 | tf_op jit(solution)/shard_map/all_to_all | solution.py:65
  20.4 32.1 %convert_multiply_fusion = f32[3,4096,2048]{2,1,0:T(8,128)} fusion(s32[3,4096]{1,0:T(4,128)} %param.6, s32[3,2048]{1,0:T(4,128)} %param.7), kind=kLoop, calls=%fused_computation | loop fusion | flops 75497472 | bytes 100737024 | tf_op jit(solution)/shard_map/mul | solution.py:25
  52.5 124.3 %fusion.8 = (bf16[4096,2048]{1,0:T(8,128)(2,1)}, f32[1,4096,2048]{2,1,0:T(8,128)S(1)}) fusion(f32[3,4096,2048]{2,1,0:T(8,128)} %convert_multiply_fusion, f32[]{:T(128)S(6)} %div.9), kind=kLoop, calls=%fused_computation.14 | loop fusion | flops 58720256 | bytes 150994944 | tf_op jit(solution)/shard_map/convert
  176.8 0.0 copy-start
  176.8 108.2 %fusion.9 = bf16[4096,2048]{1,0:T(8,128)(2,1)} fusion(f32[1,4096,2048]{2,1,0:T(8,128)S(1)} %get-tuple-element.6), kind=kLoop, calls=%fused_computation.15 | loop fusion | flops 8388608 | bytes 50331648 | tf_op jit(solution)/shard_map/convert.1
  285.0 0.0 copy-done
  285.0 0.6 dynamic-slice
  286.2 0.0 all-to-all-done
  286.3 0.7 reshape.117
  286.9 0.1 fusion.31
  287.0 0.2 copy.8
  287.2 0.5 squeeze.7
  287.7 0.2 copy.9
  287.9 0.5 squeeze.8
  288.4 12.7 %fusion.13 = f32[2048]{0:T(1024)S(1)} fusion(bf16[4096,2048]{1,0:T(8,128)(2,1)} %fusion.9, bf16[4096,2048]{1,0:T(8,128)(2,1)} %get-tuple-element.5, bf16[32,4096]{1,0:T(8,128)(2,1)S(1)} %squeeze.7, bf16[32,4096]{1,0:T(8,128)(2,1)S(1)} %squeeze.8, bf16[32,4096]{1,0:T(8,128)(2,1)S(1)} %neg.14), kind=kOutput, calls=%fused_computation.17 | convolution fusion | flops 2219046912 | bytes 34349056 | tf_op jit(solution)/shard_map/dot_general | solution.py:29
  301.2 7.6 %all-reduce = f32[2048]{0:T(1024)S(1)} all-reduce(f32[2048]{0:T(1024)S(1)} %broadcast_multiply_fusion), channel_id=2, replica_groups=mesh['seg'=4,'mic'=64] {'seg'}, use_global_device_ids=true, to_apply=%region_1.2.clone | all-reduce | flops 2048 | bytes 16384
  308.8 0.7 dynamic-slice.1
  (3 shorter events, 0.1 us)
Async XLA Ops:
  6.7 279.6 %all-to-all-start = ((bf16[64,2,2048]{2,1,0:T(2,128)(2,1)}), bf16[64,2,2048]{2,1,0:T(2,128)(2,1)S(1)}, u32[]{:S(2)}, u32[]{:S(2)}) async-start(bf16[64,2,2048]{2,1,0:T(2,128)(2,1)} %reshape.116), calls=%async_computation | async-start | bytes 1048576 | tf_op jit(solution)/shard_map/all_to_all | solution.py:65
  176.8 108.2 %copy-start = (u32[256]{0:T(256)S(1)}, u32[256]{0:T(256)}, u32[]{:S(2)}) copy-start(u32[256]{0:T(256)} %constant.33) | copy-start | bytes 3076
